TPU v7x, 32 devices: a whole 2x2x4 slice. The times are simulated.
32 devices in a mesh: lat: 16 (over z, y, x), field: 2 (over core).
Axes of the slice: x: 2, y: 2, z: 4, core: 2. Of those that a mesh axis runs over, the one named last changes fastest.
Arguments:
- fields_grid: bfloat16 [2, 64, 2, 48, 192], P('field', None, None, 'lat'), may hold values from -6 to 6
- basis: bfloat16 [128, 48, 96], P('lat'), may hold values from -0.875 to 0.875
- order_table: int32 [16, 8], replicated, may hold values from -1 to 95, as said below
- panel_modes: int32 [2, 64], replicated, may hold values from 0 to 95, as said below
Outputs:
- panel: bfloat16 [2, 128, 192, 128], P('field', 'lat')
Inputs may be any that keep to these rules, and one draw needn't show every extreme that they name: `order_table`: each order 0 to 95 stands in exactly one slot; every other slot holds -1; some group has all 8 slots filled. `panel_modes`: row 1 is never smaller than row 0 in the same column; degree 95 appears.
All inputs are finite; a program needn't handle non-finite values.
Results may differ from a plain program's by a relative error of at most 0.0082.
Values may be sent and summed in bfloat16 or wider, within the bound.
A program may use at most 64 MiB of HBM per device.

v0:
```python
import math

import jax
import jax.numpy as jnp
from jax import lax
from jax.sharding import PartitionSpec as P


def dft_table(orders, lon_count):
    valid_slot = orders >= 0
    safe_orders = jnp.maximum(orders, 0)
    products = lax.broadcasted_iota(jnp.int32, (lon_count, 1), 0) * safe_orders[None, :] % lon_count
    angles = products.astype(jnp.float32) * (2.0 * math.pi / lon_count)
    cosine = jnp.where(valid_slot[None, :], jnp.cos(angles), 0.0).astype(jnp.bfloat16)
    sine_table = jnp.where(valid_slot[None, :], -jnp.sin(angles), 0.0).astype(jnp.bfloat16)
    return jnp.stack([cosine, sine_table], axis=1)


def local(fields_grid, basis, order_table, panel_modes):
    grid_one = fields_grid[0]
    snap_count = grid_one.shape[0]
    pair_count = grid_one.shape[2]
    lon_count = grid_one.shape[3]
    slot_count = order_table.shape[1]
    deg_count = basis.shape[2]
    pair_total = basis.shape[1]
    mode_count = panel_modes.shape[1]
    orders = order_table.reshape(-1)
    slot_all = orders.shape[0]
    dft = dft_table(orders, lon_count)
    fourier = jnp.einsum("thjn,nrk->hkjrt", grid_one, dft, preferred_element_type=jnp.float32) * (
        1.0 / math.sqrt(lon_count)
    )
    fourier = fourier.reshape(2, slot_all, pair_count, 2 * snap_count)
    parity_parts = jnp.stack([fourier[0] + fourier[1], fourier[0] - fourier[1]]).astype(
        jnp.bfloat16
    )
    group_index = lax.axis_index("lat")
    my_orders = lax.dynamic_slice_in_dim(order_table, group_index, 1, 0)[0]
    my_odd = my_orders % 2 == 1
    basis_split = basis.reshape(slot_count, pair_total, deg_count // 2, 2)
    even_rows = basis_split[:, :, :, 0]
    odd_rows = basis_split[:, :, :, 1]
    degree = lax.broadcasted_iota(jnp.int32, (1, deg_count), 1)
    keep_mask = (degree >= my_orders[:, None]) & (my_orders >= 0)[:, None]
    received = lax.all_to_all(parity_parts, "lat", split_axis=1, concat_axis=2, tiled=True)
    first_parity = jnp.where(my_odd[:, None, None], received[1], received[0])
    second = jnp.where(my_odd[:, None, None], received[0], received[1])
    low_degrees = jnp.einsum(
        "sjh,sjc->shc", even_rows, first_parity, preferred_element_type=jnp.float32
    )
    high_degrees = jnp.einsum("sjh,sjc->shc", odd_rows, second, preferred_element_type=jnp.float32)
    joined = jnp.stack([low_degrees, high_degrees], axis=2).reshape(slot_count, deg_count, -1)
    coefficients = jnp.where(keep_mask[:, :, None], joined, 0.0).astype(jnp.bfloat16)
    mode_order = panel_modes[0]
    mode_degree = panel_modes[1]
    onehot = (my_orders[None, :] == mode_order[:, None]).astype(jnp.bfloat16)
    picked = jnp.take(coefficients, mode_degree, axis=1)
    local_values = jnp.einsum("ms,smc->mc", onehot, picked, preferred_element_type=jnp.float32)
    field_index = lax.axis_index("field")
    both_fields = jnp.stack(
        [
            jnp.where(field_index == 0, local_values, 0.0),
            jnp.where(field_index == 1, local_values, 0.0),
        ]
    )
    summed = lax.psum(both_fields, ("lat", "field"))
    other_field = jnp.where(field_index == 0, summed[1], summed[0]).astype(jnp.bfloat16)
    columns = other_field.astype(jnp.float32).reshape(mode_count * 2, snap_count)
    centered = (columns - jnp.mean(columns, axis=1, keepdims=True)).astype(jnp.bfloat16)
    coef_rows = coefficients.reshape(slot_count * deg_count * 2, snap_count)
    panel_values = lax.dot_general(
        coef_rows, centered, (((1,), (1,)), ((), ())), preferred_element_type=jnp.float32
    )
    panel_values = panel_values * (1.0 / (snap_count - 1))
    return panel_values.astype(jnp.bfloat16).reshape(1, slot_count, 2 * deg_count, 2 * mode_count)


def solution(mesh):
    placed = (P("field", None, None, "lat", None), P("lat", None, None), P(), P())
    return jax.shard_map(
        local, mesh=mesh, in_specs=placed, out_specs=P("field", "lat", None, None), check_vma=False
    )
```

profile of v0, /device:TPU:0, one launch (start us, length us, event | category | flops | bytes accessed | tf_op | source)
XLA Modules:
  0.0 63.5 jit_solution(17050038539362757233)
XLA Ops:
  0.0 0.0 copy-start.1
  0.0 0.8 %broadcast_compare_fusion = pred[16,8]{0,1:T(8,128)(4,1)S(1)} fusion(s32[16,8]{0,1:T(8,128)} %param.6), kind=kLoop, calls=%fused_computation.57 | loop fusion | flops 128 | bytes 640 | tf_op jit(solution)/shard_map/ge | solution.py:10
  0.8 0.0 copy-done.1
  0.8 0.1 copy.39
  0.9 0.1 ge.51
  1.0 0.1 copy.40
  1.0 0.1 max.11
  1.1 0.4 select_convert_fusion.1
  1.6 1.1 %fusion.1 = f32[2,128,3,2,64]{1,4,2,0,3:T(8,128)S(1)} fusion(bf16[64,2,3,192]{3,1,2,0:T(2,128)(2,1)} %bitcast.69, bf16[192,1,128]{2,0,1:T(8,128)(2,1)S(1)} %get-tuple-element.16, bf16[192,1,128]{2,0,1:T(8,128)(2,1)S(1)} %get-tuple-element.15), kind=kOutput, calls=%fused_computation.4 | convolution fusion | flops 38043648 | bytes 638976 | tf_op jit(solution)/shard_map/thjn,nrk->hkjrt/dot_general | solution.py:31
  2.8 0.8 %copy.44 = bf16[2,128,3,128]{3,0,2,1:T(2,128)(2,1)} copy(bf16[2,128,3,128]{1,3,2,0:T(8,128)(2,1)S(1)} %pad_maximum_fusion.1) | data formatting | bytes 393216 | tf_op jit(solution)/shard_map/stack | solution.py:35
  3.7 0.0 copy-start
  3.7 8.5 %all-to-all-start = ((bf16[2,128,3,128]{3,0,2,1:T(2,128)(2,1)}), bf16[2,128,3,128]{3,0,2,1:T(2,128)(2,1)S(1)}, u32[]{:S(2)}, u32[]{:S(2)}) async-start(bf16[2,128,3,128]{3,0,2,1:T(2,128)(2,1)} %copy.44), calls=%async_computation | async-start | bytes 393216 | tf_op jit(solution)/shard_map/all_to_all | solution.py:46
  12.1 0.0 copy-start.2
  12.2 0.7 %copy-done.2 = s32[2,64]{1,0:T(2,128)S(1)} copy-done((s32[2,64]{1,0:T(2,128)S(1)}, s32[2,64]{1,0:T(2,128)}, u32[]{:S(2)}) %copy-start.2) | copy-done | bytes 536
  12.8 0.2 dynamic-slice_reduce_fusion
  13.0 0.1 compare_bitcast_fusion
  13.2 0.0 copy-done
  13.2 0.2 copy.48
  13.4 7.4 %all-to-all-done = bf16[2,128,3,128]{3,0,2,1:T(2,128)(2,1)S(1)} async-done(((bf16[2,128,3,128]{3,0,2,1:T(2,128)(2,1)}), bf16[2,128,3,128]{3,0,2,1:T(2,128)(2,1)S(1)}, u32[]{:S(2)}, u32[]{:S(2)}) %all-to-all-start) | async-done | bytes 196640 | tf_op jit(solution)/shard_map/all_to_all | solution.py:46
  20.9 0.1 bitcast_select_fusion.2
  21.0 0.2 convolution_bitcast_fusion.1
  21.2 0.2 convolution_bitcast_fusion
  21.4 0.1 copy.53
  21.5 0.2 fusion.2
  21.7 0.6 gather_fusion
  22.3 0.3 fusion.5
  22.6 39.0 %psum.7 = bf16[2,64,128]{2,1,0:T(8,128)(2,1)S(1)} all-reduce(f32[2,64,128]{2,1,0:T(8,128)S(1)} %pad_maximum_fusion.2), channel_id=1, replica_groups=mesh['lat'=16,'field'=2] {'lat','field'}, use_global_device_ids=true, to_apply=%region_0.1 | all-reduce | flops 16384 | bytes 98304 | tf_op jit(solution)/shard_map/psum | solution.py:67
  61.6 0.1 reshape.345
  61.7 0.1 reduce_sum.9
  61.8 0.1 div.10
  62.0 0.1 sub.26
  62.1 0.1 sub.27
  62.2 0.1 convert_element_type.92
  62.3 0.2 convert_element_type.86
  62.5 1.0 %fusion = bf16[1536,128]{1,0:T(8,128)(2,1)} fusion(bf16[1536,64]{1,0:T(8,128)(2,1)S(1)} %convert_element_type.86, bf16[128,64]{1,0:T(8,128)(2,1)S(1)} %convert_element_type.92), kind=kOutput, calls=%fused_computation.2 | convolution fusion | flops 25559040 | bytes 606208 | tf_op jit(solution)/shard_map/dot_general | solution.py:72
  (23 shorter events, 0.3 us)
Async XLA Ops:
  0.0 0.8 %copy-start.1 = (s32[16,8]{0,1:T(8,128)S(1)}, s32[16,8]{0,1:T(8,128)}, u32[]{:S(2)}) copy-start(s32[16,8]{0,1:T(8,128)} %param.6) | copy-start | bytes 1540
  3.7 9.5 %copy-start = (bf16[8,48,96]{2,1,0:T(8,128)(2,1)S(1)}, bf16[8,48,96]{2,1,0:T(8,128)(2,1)}, u32[]{:S(2)}) copy-start(bf16[8,48,96]{2,1,0:T(8,128)(2,1)} %param.5) | copy-start | bytes 221188
  3.7 17.1 %all-to-all-start = ((bf16[2,128,3,128]{3,0,2,1:T(2,128)(2,1)}), bf16[2,128,3,128]{3,0,2,1:T(2,128)(2,1)S(1)}, u32[]{:S(2)}, u32[]{:S(2)}) async-start(bf16[2,128,3,128]{3,0,2,1:T(2,128)(2,1)} %copy.44), calls=%async_computation | async-start | bytes 393216 | tf_op jit(solution)/shard_map/all_to_all | solution.py:46
  12.1 0.7 %copy-start.2 = (s32[2,64]{1,0:T(2,128)S(1)}, s32[2,64]{1,0:T(2,128)}, u32[]{:S(2)}) copy-start(s32[2,64]{1,0:T(2,128)} %param.7) | copy-start | bytes 1540
where the time goes:
time: 63.9 us; the launch traced here: 63.5 us
  blocking collectives  39 us (61%)
  starting transfers between devices  8.47 us (13%)
  waiting for transfers between devices  7.41 us (12%)
  local copies, waits for them, and re-layouts  3.74 us (6%)
  matrix products  2.79 us (4%)
  other arithmetic  1.84 us (3%)
    psum x1, blocking collectives, local(): summed = lax.psum(both_fields, ('lat', 'field'))  39 us
    all_to_all x1, starting transfers between devices, local(): lax.all_to_all(parity_parts, 'lat', split_axis=1, concat_axis=2, tiled=True)  8.47 us
    all_to_all x1, waiting for transfers between devices, local(): lax.all_to_all(parity_parts, 'lat', split_axis=1, concat_axis=2, tiled=True)  7.41 us
  transfers between devices with their start and end apart: 1, of which 1 were waited for; matrix products, arithmetic and copies ran while one was open for 1% of the time, Pallas kernels for 0%

commit v1 on v0

--- a/solution.py
+++ b/solution.py
@@ -1,9 +1,257 @@
+import functools
 import math
 
 import jax
 import jax.numpy as jnp
+import numpy as np
 from jax import lax
+from jax.experimental import pallas as pl
+from jax.experimental.pallas import tpu as pltpu
 from jax.sharding import PartitionSpec as P
+
+BF = jnp.bfloat16
+F32 = jnp.float32
+NT = (((1,), (1,)), ((), ()))
+
+
+def iota(shape, dim):
+    return lax.broadcasted_iota(jnp.int32, shape, dim)
+
+
+def mm(a, b):
+    return jnp.dot(a, b, preferred_element_type=F32)
+
+
+def mm_nt(a, b):
+    return lax.dot_general(a, b, NT, preferred_element_type=F32)
+
+
+def kernel(
+    lat_count, snap, pairs, lon, slots, degs, per_dev, tail,
+    orders_ref, x_ref, basis_ref, table_ref, cols_ref, row_ref,
+    out_ref,
+    send, recv, mode_send, mode_recv, perm, rows,
+    send_sem, recv_sem, mode_send_sem, mode_recv_sem,
+):
+    me = lax.axis_index("lat")
+    field = lax.axis_index("field")
+    other = 1 - field
+    pair_total = lat_count * pairs
+    width = 2 * snap
+    block = 2 * slots
+    head = pairs * block
+    all_rows = lat_count * block
+    tail_rows = lat_count * tail
+    used = pairs * per_dev
+
+    barrier = pltpu.get_barrier_semaphore()
+
+    def greet_own(k, c):
+        pl.semaphore_signal(barrier, inc=1, device_id=(lax.rem(me + k, lat_count), field),
+                            device_id_type=pl.DeviceIdType.MESH)
+        return c
+
+    def greet_other(k, c):
+        pl.semaphore_signal(barrier, inc=1, device_id=(lax.rem(me + k, lat_count), other),
+                            device_id_type=pl.DeviceIdType.MESH)
+        return c
+
+    lax.fori_loop(1, lat_count, greet_own, 0)
+    lax.fori_loop(0, lat_count, greet_other, 0)
+
+    order_col = cols_ref[:, 0:1]
+    mode_col = cols_ref[:, 1:2]
+    deg_col = cols_ref[:, 2:3]
+    nord = table_ref.shape[0] // 2
+    parity_row = iota((all_rows, 1), 0) // slots % 2
+    want = jnp.where(order_col >= 0, order_col + nord * parity_row, -1)
+    onehot = (iota((all_rows, 2 * nord), 1) == want).astype(F32).astype(BF)
+    dft = mm(onehot, table_ref[...]).astype(BF)
+    rho = iota((tail_rows, 1), 0) % tail
+    row_order = row_ref[...]
+    row_parity = iota((1, all_rows), 1) // slots % 2
+    mode_parity = (deg_col - mode_col) % 2
+    match = (mode_col == row_order) & (mode_parity == row_parity)
+    tail_acc = jnp.zeros((tail_rows, width), F32)
+    zero_x = jnp.zeros((snap, 2 * lon), BF)
+    for j in range(pairs):
+        xj = x_ref[j]
+        both = jnp.concatenate(
+            [jnp.concatenate([xj, zero_x], axis=1), jnp.concatenate([zero_x, xj], axis=1)], axis=0
+        )
+        part = (mm_nt(dft, both) * (1.0 / math.sqrt(lon))).astype(BF)
+        send[:, j * block:(j + 1) * block, :] = part.reshape(lat_count, block, width)
+        mine = match & (rho // per_dev == j)
+        tail_acc = tail_acc + mm(mine.astype(F32).astype(BF), part)
+    at_degree = (iota((tail_rows, degs), 1) == deg_col) & (rho >= used) & (rho < used + per_dev)
+    basis_acc = jnp.zeros((tail_rows, pair_total), F32)
+    for s in range(slots):
+        pick = at_degree & (mode_col == orders_ref[me, s])
+        basis_acc = basis_acc + mm_nt(pick.astype(F32).astype(BF), basis_ref[s])
+    wide = jnp.concatenate(
+        [basis_acc, jnp.zeros((tail_rows, width - pair_total), F32)], axis=1
+    )
+    tail_all = (tail_acc + wide).astype(BF)
+    send[:, head:head + tail, :] = tail_all.reshape(lat_count, tail, width)
+
+    pl.semaphore_wait(barrier, 2 * lat_count - 1)
+
+    def block_copy(dst, src):
+        return pltpu.make_async_remote_copy(
+            src_ref=send.at[dst], dst_ref=recv.at[src],
+            send_sem=send_sem.at[dst], recv_sem=recv_sem.at[src],
+            device_id=(dst, field), device_id_type=pl.DeviceIdType.MESH,
+        )
+
+    def start_block(k, c):
+        block_copy(lax.rem(me + k, lat_count), me).start()
+        return c
+
+    lax.fori_loop(1, lat_count, start_block, 0)
+    recv[me] = send[me]
+
+    k_rows = slots * 2 * pair_total
+    for s in range(slots):
+        shape = (2 * pair_total, k_rows // 1)
+        r = iota((2 * pair_total, 1), 0)
+        p = r // pair_total
+        j = r % pair_total
+        target = j * block + p * slots + s
+        perm[s * 2 * pair_total:(s + 1) * 2 * pair_total, :] = (
+            iota((2 * pair_total, lat_count * head), 1) == target
+        ).astype(F32).astype(BF)
+    dup = (iota((2 * degs, degs), 0) // 2 == iota((2 * degs, degs), 1)).astype(F32).astype(BF)
+    for s in range(slots):
+        order = orders_ref[me, s]
+        deg = iota((2 * degs, pair_total), 0) // 2
+        base = mm_nt(dup, basis_ref[s])
+        keep = (deg >= order) & (order >= 0)
+        odd = (deg - order) % 2
+        even_part = jnp.where(keep & (odd == 0), base, 0.0)
+        odd_part = jnp.where(keep & (odd == 1), base, 0.0)
+        rows[s] = jnp.concatenate([even_part, odd_part], axis=1).astype(BF)
+    src_of = iota((width, tail_rows), 1) // tail
+    rho_of = iota((width, tail_rows), 1) % tail
+    spread = (
+        (iota((width, tail_rows), 0) == src_of * pairs + rho_of // per_dev) & (rho_of < used)
+    ).astype(F32).astype(BF)
+    own_row = iota((tail, tail_rows), 0) - used == iota((tail, tail_rows), 1) % tail % per_dev
+
+    def wait_block(k, c):
+        src = lax.rem(me + k, lat_count)
+        block_copy(src, src).wait_recv()
+        return c
+
+    lax.fori_loop(1, lat_count, wait_block, 0)
+
+    tails = recv[:, head:head + tail, :]
+    summed = jnp.sum(tails.astype(F32), axis=0).astype(BF)
+    weights = jnp.where(own_row, mm(summed, spread), 0.0).astype(BF)
+    mode_send[...] = mm(weights, tails.reshape(tail_rows, width)).astype(BF)
+
+    def mode_copy(dst, src):
+        return pltpu.make_async_remote_copy(
+            src_ref=mode_send, dst_ref=mode_recv.at[src],
+            send_sem=mode_send_sem.at[dst], recv_sem=mode_recv_sem.at[src],
+            device_id=(dst, other), device_id_type=pl.DeviceIdType.MESH,
+        )
+
+    def start_mode(k, c):
+        mode_copy(lax.rem(me + k, lat_count), me).start()
+        return c
+
+    lax.fori_loop(0, lat_count, start_mode, 0)
+
+    heads = recv[:, 0:head, :].reshape(lat_count * head, width)
+    sorted_rows = mm(perm[...], heads).astype(BF)
+    same_r = iota((2 * degs, width), 1) // snap == iota((2 * degs, width), 0) % 2
+    coefs = []
+    for s in range(slots):
+        value = mm(rows[s], sorted_rows[s * 2 * pair_total:(s + 1) * 2 * pair_total])
+        coefs.append(jnp.where(same_r, value, 0.0).astype(BF))
+
+    modes = lat_count * per_dev
+    cu = iota((2 * modes, tail_rows), 0)
+    mode_at = cu // 2 // per_dev * tail + used + cu // 2 % per_dev
+    expand = (iota((2 * modes, tail_rows), 1) == mode_at).astype(F32).astype(BF)
+
+    def wait_mode(k, c):
+        src = lax.rem(me + k, lat_count)
+        mode_copy(src, src).wait_recv()
+        return c
+
+    lax.fori_loop(0, lat_count, wait_mode, 0)
+    values = mode_recv[...].reshape(tail_rows, width)
+    columns = mm(expand, values)
+    u_match = iota((2 * modes, width), 1) // snap == iota((2 * modes, width), 0) % 2
+    masked = jnp.where(u_match, columns, 0.0)
+    mean = jnp.sum(masked, axis=1, keepdims=True) * (1.0 / snap)
+    centered = jnp.where(u_match, masked - mean, 0.0)
+    twice = (centered + pltpu.roll(centered, snap, 1)).astype(BF)
+    for s in range(slots):
+        out_ref[s] = (mm_nt(coefs[s], twice) * (1.0 / (snap - 1))).astype(BF)
+
+    def finish(k, c):
+        dst = lax.rem(me + k, lat_count)
+        block_copy(dst, dst).wait_send()
+        return c
+
+    def finish_mode(k, c):
+        dst = lax.rem(me + k, lat_count)
+        mode_copy(dst, dst).wait_send()
+        return c
+
+    lax.fori_loop(1, lat_count, finish, 0)
+    lax.fori_loop(0, lat_count, finish_mode, 0)
+
+
+def dft_constant(nord, lon):
+    angles = (np.outer(np.arange(nord), np.arange(lon)) % lon) * (2.0 * math.pi / lon)
+    cosine, sine = np.cos(angles), -np.sin(angles)
+    even = np.concatenate([cosine, cosine, sine, sine], axis=1)
+    odd = np.concatenate([cosine, -cosine, sine, -sine], axis=1)
+    return np.concatenate([even, odd], axis=0).astype(np.float32).astype(BF)
+
+
+def fused(lat_count, tail, fields_grid, basis, order_table, panel_modes):
+    _, snap, _, pairs, lon = fields_grid.shape
+    slots, pair_total, degs = basis.shape
+    modes = panel_modes.shape[1]
+    per_dev = modes // lat_count
+    width = 2 * snap
+    block = 2 * slots
+    head = pairs * block
+    x = fields_grid[0].transpose(2, 0, 1, 3).reshape(pairs, snap, 2 * lon)
+    by_row = jnp.broadcast_to(order_table[:, None, :], (lat_count, 2, slots)).reshape(-1)
+    padded = jnp.broadcast_to(
+        panel_modes.reshape(2, lat_count, 1, per_dev), (2, lat_count, tail // per_dev, per_dev)
+    ).reshape(2, -1)
+    cols = jnp.concatenate([by_row[None], padded], axis=0).T
+    table = jnp.asarray(dft_constant(degs, lon))
+    vmem = pl.BlockSpec(memory_space=pltpu.VMEM)
+    body = functools.partial(kernel, lat_count, snap, pairs, lon, slots, degs, per_dev, tail)
+    out = pl.pallas_call(
+        body,
+        out_shape=jax.ShapeDtypeStruct((slots, 2 * degs, 2 * modes), BF),
+        in_specs=[pl.BlockSpec(memory_space=pltpu.SMEM)] + [vmem] * 5,
+        out_specs=vmem,
+        scratch_shapes=[
+            pltpu.VMEM((lat_count, head + tail, width), BF),
+            pltpu.VMEM((lat_count, head + tail, width), BF),
+            pltpu.VMEM((tail, width), BF),
+            pltpu.VMEM((lat_count, tail, width), BF),
+            pltpu.VMEM((slots * 2 * pair_total, lat_count * head), BF),
+            pltpu.VMEM((slots, 2 * degs, 2 * pair_total), BF),
+            pltpu.SemaphoreType.DMA((lat_count,)),
+            pltpu.SemaphoreType.DMA((lat_count,)),
+            pltpu.SemaphoreType.DMA((lat_count,)),
+            pltpu.SemaphoreType.DMA((lat_count,)),
+        ],
+        compiler_params=pltpu.CompilerParams(
+            collective_id=0, has_side_effects=True, vmem_limit_bytes=48 * 1024 * 1024
+        ),
+    )(order_table, x, basis, table, cols, by_row[None])
+    return out[None]
 
 
 def dft_table(orders, lon_count):
@@ -76,8 +324,29 @@
     return panel_values.astype(jnp.bfloat16).reshape(1, slot_count, 2 * deg_count, 2 * mode_count)
 
 
+def device_program(lat_count, fields_grid, basis, order_table, panel_modes):
+    pairs, snap = fields_grid.shape[3], fields_grid.shape[1]
+    slots, pair_total, _ = basis.shape
+    modes = panel_modes.shape[1]
+    per_dev = modes // lat_count
+    tail = (pairs + 1) * per_dev if per_dev else 0
+    rows = slots * 2 * pair_total
+    fits = (
+        modes % lat_count == 0
+        and tail == 2 * slots
+        and tail % 16 == 0
+        and 2 * snap == 128
+        and pair_total <= 2 * snap
+        and rows * rows * 2 <= 8 * 1024 * 1024
+    )
+    if fits:
+        return fused(lat_count, tail, fields_grid, basis, order_table, panel_modes)
+    return local(fields_grid, basis, order_table, panel_modes)
+
+
 def solution(mesh):
     placed = (P("field", None, None, "lat", None), P("lat", None, None), P(), P())
     return jax.shard_map(
-        local, mesh=mesh, in_specs=placed, out_specs=P("field", "lat", None, None), check_vma=False
-    )
+        functools.partial(device_program, mesh.shape["lat"]),
+        mesh=mesh, in_specs=placed, out_specs=P("field", "lat", None, None), check_vma=False,
+    )

time: 63.9 us -> 26.2 us (0.41)
  the two profiles are of different devices: /device:TPU:0 before, /device:TPU:1 now
where the time goes in v1:
time: 26.2 us; the launch traced here: 26 us
  Pallas kernels  22.1 us (84%)
  local copies, waits for them, and re-layouts  3.81 us (15%)
    pallas_call x1, Pallas kernels, fused(): pl.pallas_call(body, out_shape=jax.ShapeDtypeStruct((slots, 2 * degs, 2 *...  22.1 us
    unnamed x8, local copies, waits for them, and re-layouts  2.44 us
    broadcast_in_dim x2, local copies, waits for them, and re-layouts, fused(): jnp.broadcast_to(panel_modes.reshape(2, lat_count, 1, per_dev), (2, lat_c...  0.78 us

profile of v1, /device:TPU:1, one launch (start us, length us, event | category | flops | bytes accessed | tf_op | source)
XLA Modules:
  0.0 26.0 jit_solution(4723037578172791840)
XLA Ops:
  0.0 0.0 copy-start.2
  0.0 0.8 %copy.23.orders_ref = s32[16,8]{1,0:T(8,128)S(1)} copy(s32[16,8]{0,1:T(8,128)} %param.7) | data formatting | bytes 1024 | tf_op args[2]
  0.8 0.1 broadcast_in_dim_reshape.4.row_ref
  0.9 0.8 %broadcast_in_dim.17 = s32[2,16,4]{2,1,0:T(8,128)S(1)} reshape(s32[2,64]{1,0:T(2,128)} %param.8) | data formatting | bytes 1024 | tf_op jit(solution)/shard_map/broadcast_in_dim | solution.py:226
  1.7 0.1 reshape.10
  1.8 0.1 copy.22
  2.0 0.0 copy-done.2
  2.0 0.0 copy-start
  2.0 0.2 reshape.11
  2.2 0.0 copy-start.1
  2.3 0.7 %copy-done = bf16[192,768]{1,0:T(8,128)(2,1)S(1)} copy-done((bf16[192,768]{1,0:T(8,128)(2,1)S(1)}, bf16[192,768]{1,0:T(8,128)(2,1)}, u32[]{:S(2)}) %copy-start) | copy-done | bytes 294936
  2.9 0.2 copy-done.1
  3.1 22.1 %shard_map.55 = bf16[8,192,128]{2,1,0:T(8,128)(2,1)S(1)} custom-call(s32[16,8]{1,0:T(8,128)S(1)} %copy.23.orders_ref, bf16[3,64,384]{2,1,0:T(8,128)(2,1)S(1)} %copy.24.x_ref, bf16[8,48,96]{2,1,0:T(8,128)(2,1)S(1)} %copy-done.1, bf16[192,768]{1,0:T(8,128)(2,1)S(1)} %copy-done, s32[256,3]{1,0:T(8,128)S(1)} %bitcast.8, s32[1,256]{1,0:T(1,128)S(1)} %broadcast_in_dim_reshape.4.row_ref), custom_call_target="tpu_custom_call" | custom-call | tf_op jit(solution)/shard_map/pallas_call | solution.py:233
  25.2 0.7 %copy.26 = bf16[1,8,192,128]{3,2,1,0:T(8,128)(2,1)} copy(bf16[1,8,192,128]{3,2,1,0:T(8,128)(2,1)S(1)} %bitcast.7) | data formatting | bytes 786432
  (4 shorter events, 0.1 us)
Async XLA Ops:
  0.0 2.0 %copy-start.2 = (bf16[1,64,2,3,192]{4,2,3,1,0:T(2,128)(2,1)S(1)}, bf16[1,64,2,3,192]{4,2,3,1,0:T(2,128)(2,1)}, u32[]{:S(2)}) copy-start(bf16[1,64,2,3,192]{4,2,3,1,0:T(2,128)(2,1)} %param.5) | copy-start | bytes 442372
  2.0 1.0 %copy-start = (bf16[192,768]{1,0:T(8,128)(2,1)S(1)}, bf16[192,768]{1,0:T(8,128)(2,1)}, u32[]{:S(2)}) copy-start(bf16[192,768]{1,0:T(8,128)(2,1)} %constant.2.clone.table_ref) | copy-start | bytes 884740
  2.2 0.9 %copy-start.1 = (bf16[8,48,96]{2,1,0:T(8,128)(2,1)S(1)}, bf16[8,48,96]{2,1,0:T(8,128)(2,1)}, u32[]{:S(2)}) copy-start(bf16[8,48,96]{2,1,0:T(8,128)(2,1)} %basis_ref.1) | copy-start | bytes 221188

commit v2 on v1

--- a/solution.py
+++ b/solution.py
@@ -28,8 +28,9 @@
 
 def kernel(
     lat_count, snap, pairs, lon, slots, degs, per_dev, tail,
-    orders_ref, x_ref, basis_ref, table_ref, cols_ref, row_ref,
+    x_hbm, basis_hbm, table_hbm, orders_hbm, modes_hbm,
     out_ref,
+    x_ref, basis_ref, table_ref, orders_ref, modes_ref, load_sem,
     send, recv, mode_send, mode_recv, perm, rows,
     send_sem, recv_sem, mode_send_sem, mode_recv_sem,
 ):
@@ -44,6 +45,16 @@
     tail_rows = lat_count * tail
     used = pairs * per_dev
 
+    loads = [
+        pltpu.make_async_copy(src, dst, load_sem.at[at])
+        for at, (src, dst) in enumerate([
+            (orders_hbm, orders_ref), (modes_hbm, modes_ref), (table_hbm, table_ref),
+            (x_hbm, x_ref), (basis_hbm, basis_ref),
+        ])
+    ]
+    for load in loads:
+        load.start()
+
     barrier = pltpu.get_barrier_semaphore()
 
     def greet_own(k, c):
@@ -59,23 +70,39 @@
     lax.fori_loop(1, lat_count, greet_own, 0)
     lax.fori_loop(0, lat_count, greet_other, 0)
 
-    order_col = cols_ref[:, 0:1]
-    mode_col = cols_ref[:, 1:2]
-    deg_col = cols_ref[:, 2:3]
     nord = table_ref.shape[0] // 2
+    loads[0].wait()
+    loads[1].wait()
+    by_slot = orders_ref[...]
+    tiled = jnp.concatenate([by_slot] * (2 * lat_count), axis=0)
+    here = iota((all_rows, lat_count), 1) == iota((all_rows, lat_count), 0) // block
+    order_col = jnp.sum(jnp.where(here, tiled, 0), axis=1, keepdims=True)
+    mode_total = lat_count * per_dev
+    mode_row = iota((tail_rows, mode_total), 0)
+    mode_here = iota((tail_rows, mode_total), 1) == mode_row // tail * per_dev + mode_row % per_dev
+    mode_col = jnp.sum(jnp.where(mode_here, modes_ref[0:1, :], 0), axis=1, keepdims=True)
+    deg_col = jnp.sum(jnp.where(mode_here, modes_ref[1:2, :], 0), axis=1, keepdims=True)
+    my_orders = jnp.sum(
+        jnp.where(iota((slots, lat_count), 1) == me, by_slot, 0), axis=1, keepdims=True
+    )
+    group_of = (iota((lat_count, all_rows), 1) // block == iota((lat_count, all_rows), 0))
+    by_lane = mm(by_slot.astype(F32).astype(BF), group_of.astype(F32).astype(BF))
+    slot_of = iota((slots, all_rows), 1) % slots == iota((slots, all_rows), 0)
+    row_order = jnp.sum(jnp.where(slot_of, by_lane, 0.0), axis=0, keepdims=True).astype(jnp.int32)
     parity_row = iota((all_rows, 1), 0) // slots % 2
     want = jnp.where(order_col >= 0, order_col + nord * parity_row, -1)
     onehot = (iota((all_rows, 2 * nord), 1) == want).astype(F32).astype(BF)
+    loads[2].wait()
     dft = mm(onehot, table_ref[...]).astype(BF)
     rho = iota((tail_rows, 1), 0) % tail
-    row_order = row_ref[...]
     row_parity = iota((1, all_rows), 1) // slots % 2
     mode_parity = (deg_col - mode_col) % 2
     match = (mode_col == row_order) & (mode_parity == row_parity)
     tail_acc = jnp.zeros((tail_rows, width), F32)
     zero_x = jnp.zeros((snap, 2 * lon), BF)
+    loads[3].wait()
     for j in range(pairs):
-        xj = x_ref[j]
+        xj = jnp.concatenate([x_ref[:, j, 0, :], x_ref[:, j, 1, :]], axis=1)
         both = jnp.concatenate(
             [jnp.concatenate([xj, zero_x], axis=1), jnp.concatenate([zero_x, xj], axis=1)], axis=0
         )
@@ -84,9 +111,10 @@
         mine = match & (rho // per_dev == j)
         tail_acc = tail_acc + mm(mine.astype(F32).astype(BF), part)
     at_degree = (iota((tail_rows, degs), 1) == deg_col) & (rho >= used) & (rho < used + per_dev)
+    loads[4].wait()
     basis_acc = jnp.zeros((tail_rows, pair_total), F32)
     for s in range(slots):
-        pick = at_degree & (mode_col == orders_ref[me, s])
+        pick = at_degree & (mode_col == my_orders[s:s + 1, :])
         basis_acc = basis_acc + mm_nt(pick.astype(F32).astype(BF), basis_ref[s])
     wide = jnp.concatenate(
         [basis_acc, jnp.zeros((tail_rows, width - pair_total), F32)], axis=1
@@ -122,7 +150,7 @@
         ).astype(F32).astype(BF)
     dup = (iota((2 * degs, degs), 0) // 2 == iota((2 * degs, degs), 1)).astype(F32).astype(BF)
     for s in range(slots):
-        order = orders_ref[me, s]
+        order = my_orders[s:s + 1, :]
         deg = iota((2 * degs, pair_total), 0) // 2
         base = mm_nt(dup, basis_ref[s])
         keep = (deg >= order) & (order >= 0)
@@ -221,21 +249,22 @@
     width = 2 * snap
     block = 2 * slots
     head = pairs * block
-    x = fields_grid[0].transpose(2, 0, 1, 3).reshape(pairs, snap, 2 * lon)
-    by_row = jnp.broadcast_to(order_table[:, None, :], (lat_count, 2, slots)).reshape(-1)
-    padded = jnp.broadcast_to(
-        panel_modes.reshape(2, lat_count, 1, per_dev), (2, lat_count, tail // per_dev, per_dev)
-    ).reshape(2, -1)
-    cols = jnp.concatenate([by_row[None], padded], axis=0).T
+    x = fields_grid[0].transpose(0, 2, 1, 3)
     table = jnp.asarray(dft_constant(degs, lon))
     vmem = pl.BlockSpec(memory_space=pltpu.VMEM)
     body = functools.partial(kernel, lat_count, snap, pairs, lon, slots, degs, per_dev, tail)
     out = pl.pallas_call(
         body,
         out_shape=jax.ShapeDtypeStruct((slots, 2 * degs, 2 * modes), BF),
-        in_specs=[pl.BlockSpec(memory_space=pltpu.SMEM)] + [vmem] * 5,
+        in_specs=[pl.BlockSpec(memory_space=pl.ANY)] * 5,
         out_specs=vmem,
         scratch_shapes=[
+            pltpu.VMEM(x.shape, BF),
+            pltpu.VMEM(basis.shape, BF),
+            pltpu.VMEM(table.shape, BF),
+            pltpu.VMEM((slots, lat_count), jnp.int32),
+            pltpu.VMEM(panel_modes.shape, jnp.int32),
+            pltpu.SemaphoreType.DMA((5,)),
             pltpu.VMEM((lat_count, head + tail, width), BF),
             pltpu.VMEM((lat_count, head + tail, width), BF),
             pltpu.VMEM((tail, width), BF),
@@ -248,9 +277,9 @@
             pltpu.SemaphoreType.DMA((lat_count,)),
         ],
         compiler_params=pltpu.CompilerParams(
-            collective_id=0, has_side_effects=True, vmem_limit_bytes=48 * 1024 * 1024
+            collective_id=0, has_side_effects=True, vmem_limit_bytes=63 * 1024 * 1024
         ),
-    )(order_table, x, basis, table, cols, by_row[None])
+    )(x, basis, table, order_table.T, panel_modes)
     return out[None]
 
 
@@ -336,6 +365,8 @@
         and tail == 2 * slots
         and tail % 16 == 0
         and 2 * snap == 128
+        and slots == 8
+        and basis.shape[2] <= 256
         and pair_total <= 2 * snap
         and rows * rows * 2 <= 8 * 1024 * 1024
     )

time: 26.2 us -> 24.3 us (0.927)
  local copies, waits for them, and re-layouts: 3.81 us -> 1.77 us
  Pallas kernels: 22.1 us -> 22.4 us
    broadcast_in_dim x3 -> x0, local copies, waits for them, and re-layouts: 0.79 us -> none  [the longest x2 0.78 us: fused(): jnp.broadcast_to(panel_modes.reshape(2, lat_count, 1, per_dev), (2, lat_c...]
    unnamed x8 -> x1, local copies, waits for them, and re-layouts: 2.44 us -> 1.77 us
    reshape x3 -> x0, local copies, waits for them, and re-layouts: 0.36 us -> none  [the longest x2 0.24 us: fused(): x = fields_grid[0].transpose(2, 0, 1, 3).reshape(pairs, snap, 2 * lon)]
    pallas_call x1, Pallas kernels: 22.1 us -> 22.4 us  [fused(): pl.pallas_call(body, out_shape=jax.ShapeDtypeStruct((slots, 2 * degs, 2 *...]
where the time goes in v2:
time: 24.3 us; the launch traced here: 24.2 us
  Pallas kernels  22.4 us (92%)
  local copies, waits for them, and re-layouts  1.77 us (7%)
    pallas_call x1, Pallas kernels, fused(): pl.pallas_call(body, out_shape=jax.ShapeDtypeStruct((slots, 2 * degs, 2 *...  22.4 us
    unnamed x1, local copies, waits for them, and re-layouts  1.77 us

profile of v2, /device:TPU:1, one launch (start us, length us, event | category | flops | bytes accessed | tf_op | source)
XLA Modules:
  0.0 24.2 jit_solution(16863220429722166623)
XLA Ops:
  0.0 22.4 %shard_map.55 = bf16[8,192,128]{2,1,0:T(8,128)(2,1)} custom-call(bf16[64,3,2,192]{3,2,1,0:T(2,128)(2,1)} %bitcast.6, bf16[8,48,96]{2,1,0:T(8,128)(2,1)} %basis_hbm.1, bf16[192,768]{1,0:T(8,128)(2,1)} %constant.2.clone.table_hbm, s32[8,16]{1,0:T(8,128)} %bitcast.7, s32[2,64]{1,0:T(2,128)} %modes_hbm.1), custom_call_target="tpu_custom_call" | custom-call | tf_op jit(solution)/shard_map/pallas_call | solution.py:256
  22.4 1.8 %copy.7 = bf16[1,8,192,128]{3,2,1,0:T(8,128)(2,1)} copy(bf16[1,8,192,128]{3,2,1,0:T(8,128)(2,1)} %bitcast.5) | data formatting | bytes 786432

commit v3 on v2

--- a/solution.py
+++ b/solution.py
@@ -29,10 +29,10 @@
 def kernel(
     lat_count, snap, pairs, lon, slots, degs, per_dev, tail,
     x_hbm, basis_hbm, table_hbm, orders_hbm, modes_hbm,
-    out_ref,
+    coef_hbm, twice_ref,
     x_ref, basis_ref, table_ref, orders_ref, modes_ref, load_sem,
-    send, recv, mode_send, mode_recv, perm, rows,
-    send_sem, recv_sem, mode_send_sem, mode_recv_sem,
+    send, recv, tail_send, tail_recv, mode_send, mode_recv, perm, rows, coef, coef_sem,
+    send_sem, recv_sem, tail_send_sem, tail_recv_sem, mode_send_sem, mode_recv_sem,
 ):
     me = lax.axis_index("lat")
     field = lax.axis_index("field")
@@ -120,7 +120,7 @@
         [basis_acc, jnp.zeros((tail_rows, width - pair_total), F32)], axis=1
     )
     tail_all = (tail_acc + wide).astype(BF)
-    send[:, head:head + tail, :] = tail_all.reshape(lat_count, tail, width)
+    tail_send[...] = tail_all.reshape(lat_count, tail, width)
 
     pl.semaphore_wait(barrier, 2 * lat_count - 1)
 
@@ -131,12 +131,33 @@
             device_id=(dst, field), device_id_type=pl.DeviceIdType.MESH,
         )
 
+    def tail_copy(dst, src):
+        return pltpu.make_async_remote_copy(
+            src_ref=tail_send.at[dst], dst_ref=tail_recv.at[src],
+            send_sem=tail_send_sem.at[dst], recv_sem=tail_recv_sem.at[src],
+            device_id=(dst, field), device_id_type=pl.DeviceIdType.MESH,
+        )
+
+    def start_tail(k, c):
+        tail_copy(lax.rem(me + k, lat_count), me).start()
+        return c
+
+    lax.fori_loop(1, lat_count, start_tail, 0)
+
     def start_block(k, c):
         block_copy(lax.rem(me + k, lat_count), me).start()
         return c
 
     lax.fori_loop(1, lat_count, start_block, 0)
     recv[me] = send[me]
+    tail_recv[me] = tail_send[me]
+
+    src_of = iota((width, tail_rows), 1) // tail
+    rho_of = iota((width, tail_rows), 1) % tail
+    spread = (
+        (iota((width, tail_rows), 0) == src_of * pairs + rho_of // per_dev) & (rho_of < used)
+    ).astype(F32).astype(BF)
+    own_row = iota((tail, tail_rows), 0) - used == iota((tail, tail_rows), 1) % tail % per_dev
 
     k_rows = slots * 2 * pair_total
     for s in range(slots):
@@ -158,21 +179,14 @@
         even_part = jnp.where(keep & (odd == 0), base, 0.0)
         odd_part = jnp.where(keep & (odd == 1), base, 0.0)
         rows[s] = jnp.concatenate([even_part, odd_part], axis=1).astype(BF)
-    src_of = iota((width, tail_rows), 1) // tail
-    rho_of = iota((width, tail_rows), 1) % tail
-    spread = (
-        (iota((width, tail_rows), 0) == src_of * pairs + rho_of // per_dev) & (rho_of < used)
-    ).astype(F32).astype(BF)
-    own_row = iota((tail, tail_rows), 0) - used == iota((tail, tail_rows), 1) % tail % per_dev
-
-    def wait_block(k, c):
+    def wait_tail(k, c):
         src = lax.rem(me + k, lat_count)
-        block_copy(src, src).wait_recv()
-        return c
-
-    lax.fori_loop(1, lat_count, wait_block, 0)
-
-    tails = recv[:, head:head + tail, :]
+        tail_copy(src, src).wait_recv()
+        return c
+
+    lax.fori_loop(1, lat_count, wait_tail, 0)
+
+    tails = tail_recv[...]
     summed = jnp.sum(tails.astype(F32), axis=0).astype(BF)
     weights = jnp.where(own_row, mm(summed, spread), 0.0).astype(BF)
     mode_send[...] = mm(weights, tails.reshape(tail_rows, width)).astype(BF)
@@ -190,13 +204,21 @@
 
     lax.fori_loop(0, lat_count, start_mode, 0)
 
-    heads = recv[:, 0:head, :].reshape(lat_count * head, width)
+    def wait_block(k, c):
+        src = lax.rem(me + k, lat_count)
+        block_copy(src, src).wait_recv()
+        return c
+
+    lax.fori_loop(1, lat_count, wait_block, 0)
+
+    heads = recv[...].reshape(lat_count * head, width)
     sorted_rows = mm(perm[...], heads).astype(BF)
     same_r = iota((2 * degs, width), 1) // snap == iota((2 * degs, width), 0) % 2
-    coefs = []
     for s in range(slots):
         value = mm(rows[s], sorted_rows[s * 2 * pair_total:(s + 1) * 2 * pair_total])
-        coefs.append(jnp.where(same_r, value, 0.0).astype(BF))
+        coef[s] = jnp.where(same_r, value, 0.0).astype(BF)
+    coef_out = pltpu.make_async_copy(coef, coef_hbm, coef_sem)
+    coef_out.start()
 
     modes = lat_count * per_dev
     cu = iota((2 * modes, tail_rows), 0)
@@ -215,13 +237,13 @@
     masked = jnp.where(u_match, columns, 0.0)
     mean = jnp.sum(masked, axis=1, keepdims=True) * (1.0 / snap)
     centered = jnp.where(u_match, masked - mean, 0.0)
-    twice = (centered + pltpu.roll(centered, snap, 1)).astype(BF)
-    for s in range(slots):
-        out_ref[s] = (mm_nt(coefs[s], twice) * (1.0 / (snap - 1))).astype(BF)
+    twice_ref[...] = (centered + pltpu.roll(centered, snap, 1)).astype(BF)
+    coef_out.wait()
 
     def finish(k, c):
         dst = lax.rem(me + k, lat_count)
         block_copy(dst, dst).wait_send()
+        tail_copy(dst, dst).wait_send()
         return c
 
     def finish_mode(k, c):
@@ -253,11 +275,14 @@
     table = jnp.asarray(dft_constant(degs, lon))
     vmem = pl.BlockSpec(memory_space=pltpu.VMEM)
     body = functools.partial(kernel, lat_count, snap, pairs, lon, slots, degs, per_dev, tail)
-    out = pl.pallas_call(
+    coef, twice = pl.pallas_call(
         body,
-        out_shape=jax.ShapeDtypeStruct((slots, 2 * degs, 2 * modes), BF),
+        out_shape=(
+            jax.ShapeDtypeStruct((slots, 2 * degs, width), BF),
+            jax.ShapeDtypeStruct((2 * modes, width), BF),
+        ),
         in_specs=[pl.BlockSpec(memory_space=pl.ANY)] * 5,
-        out_specs=vmem,
+        out_specs=(pl.BlockSpec(memory_space=pl.ANY), vmem),
         scratch_shapes=[
             pltpu.VMEM(x.shape, BF),
             pltpu.VMEM(basis.shape, BF),
@@ -265,12 +290,18 @@
             pltpu.VMEM((slots, lat_count), jnp.int32),
             pltpu.VMEM(panel_modes.shape, jnp.int32),
             pltpu.SemaphoreType.DMA((5,)),
-            pltpu.VMEM((lat_count, head + tail, width), BF),
-            pltpu.VMEM((lat_count, head + tail, width), BF),
+            pltpu.VMEM((lat_count, head, width), BF),
+            pltpu.VMEM((lat_count, head, width), BF),
+            pltpu.VMEM((lat_count, tail, width), BF),
+            pltpu.VMEM((lat_count, tail, width), BF),
             pltpu.VMEM((tail, width), BF),
             pltpu.VMEM((lat_count, tail, width), BF),
             pltpu.VMEM((slots * 2 * pair_total, lat_count * head), BF),
             pltpu.VMEM((slots, 2 * degs, 2 * pair_total), BF),
+            pltpu.VMEM((slots, 2 * degs, width), BF),
+            pltpu.SemaphoreType.DMA,
+            pltpu.SemaphoreType.DMA((lat_count,)),
+            pltpu.SemaphoreType.DMA((lat_count,)),
             pltpu.SemaphoreType.DMA((lat_count,)),
             pltpu.SemaphoreType.DMA((lat_count,)),
             pltpu.SemaphoreType.DMA((lat_count,)),
@@ -280,7 +311,10 @@
             collective_id=0, has_side_effects=True, vmem_limit_bytes=63 * 1024 * 1024
         ),
     )(x, basis, table, order_table.T, panel_modes)
-    return out[None]
+    panel = lax.dot_general(
+        coef.reshape(slots * 2 * degs, width), twice, NT, preferred_element_type=F32
+    ) * (1.0 / (snap - 1))
+    return panel.astype(BF).reshape(1, slots, 2 * degs, 2 * modes)
 
 
 def dft_table(orders, lon_count):

time: 24.3 us -> 20.7 us (0.85)
  Pallas kernels: 22.4 us -> 18.6 us
  matrix products: 0 us -> 2.01 us
  local copies, waits for them, and re-layouts: 1.77 us -> 0 us
    pallas_call x1, Pallas kernels: 22.4 us -> 18.6 us  [fused(): pl.pallas_call(body, out_shape=(jax.ShapeDtypeStruct((slots, 2 * degs, wi...]
    dot_general x0 -> x1, matrix products: none -> 2.01 us  [fused(): lax.dot_general(coef.reshape(slots * 2 * degs, width), twice, NT, preferr...]
    unnamed x1 -> x0, local copies, waits for them, and re-layouts: 1.77 us -> none
where the time goes in v3:
time: 20.7 us; the launch traced here: 20.6 us
  Pallas kernels  18.6 us (90%)
  matrix products  2.01 us (10%)
    pallas_call x1, Pallas kernels, fused(): pl.pallas_call(body, out_shape=(jax.ShapeDtypeStruct((slots, 2 * degs, wi...  18.6 us
    dot_general x1, matrix products, fused(): lax.dot_general(coef.reshape(slots * 2 * degs, width), twice, NT, preferr...  2.01 us

profile of v3, /device:TPU:1, one launch (start us, length us, event | category | flops | bytes accessed | tf_op | source)
XLA Modules:
  0.0 20.6 jit_solution(2526370144964455194)
XLA Ops:
  0.0 18.6 %shard_map.55 = (bf16[8,192,128]{2,1,0:T(8,128)(2,1)}, bf16[128,128]{1,0:T(8,128)(2,1)}) custom-call(bf16[64,3,2,192]{3,2,1,0:T(2,128)(2,1)} %bitcast.9, bf16[8,48,96]{2,1,0:T(8,128)(2,1)} %basis_hbm.1, bf16[192,768]{1,0:T(8,128)(2,1)} %constant.4.clone.table_hbm, s32[8,16]{1,0:T(8,128)} %bitcast.10, s32[2,64]{1,0:T(2,128)} %modes_hbm.1), custom_call_target="tpu_custom_call" | custom-call | tf_op jit(solution)/shard_map/pallas_call | solution.py:278
  18.6 2.0 %fusion = bf16[1536,128]{1,0:T(8,128)(2,1)} fusion(bf16[1536,128]{1,0:T(8,128)(2,1)} %bitcast.8, bf16[128,128]{1,0:T(8,128)(2,1)} %get-tuple-element.8), kind=kOutput, calls=%fused_computation.1 | convolution fusion | flops 50724864 | bytes 819200 | tf_op jit(solution)/shard_map/dot_general | solution.py:314

commit v4 on v3

--- a/solution.py
+++ b/solution.py
@@ -31,7 +31,7 @@
     x_hbm, basis_hbm, table_hbm, orders_hbm, modes_hbm,
     coef_hbm, twice_ref,
     x_ref, basis_ref, table_ref, orders_ref, modes_ref, load_sem,
-    send, recv, tail_send, tail_recv, mode_send, mode_recv, perm, rows, coef, coef_sem,
+    send, recv, tail_send, tail_recv, mode_send, mode_recv, perm, rows,
     send_sem, recv_sem, tail_send_sem, tail_recv_sem, mode_send_sem, mode_recv_sem,
 ):
     me = lax.axis_index("lat")
@@ -216,9 +216,7 @@
     same_r = iota((2 * degs, width), 1) // snap == iota((2 * degs, width), 0) % 2
     for s in range(slots):
         value = mm(rows[s], sorted_rows[s * 2 * pair_total:(s + 1) * 2 * pair_total])
-        coef[s] = jnp.where(same_r, value, 0.0).astype(BF)
-    coef_out = pltpu.make_async_copy(coef, coef_hbm, coef_sem)
-    coef_out.start()
+        coef_hbm[s] = jnp.where(same_r, value, 0.0).astype(BF)
 
     modes = lat_count * per_dev
     cu = iota((2 * modes, tail_rows), 0)
@@ -238,7 +236,6 @@
     mean = jnp.sum(masked, axis=1, keepdims=True) * (1.0 / snap)
     centered = jnp.where(u_match, masked - mean, 0.0)
     twice_ref[...] = (centered + pltpu.roll(centered, snap, 1)).astype(BF)
-    coef_out.wait()
 
     def finish(k, c):
         dst = lax.rem(me + k, lat_count)
@@ -282,7 +279,7 @@
             jax.ShapeDtypeStruct((2 * modes, width), BF),
         ),
         in_specs=[pl.BlockSpec(memory_space=pl.ANY)] * 5,
-        out_specs=(pl.BlockSpec(memory_space=pl.ANY), vmem),
+        out_specs=(vmem, vmem),
         scratch_shapes=[
             pltpu.VMEM(x.shape, BF),
             pltpu.VMEM(basis.shape, BF),
@@ -298,8 +295,6 @@
             pltpu.VMEM((lat_count, tail, width), BF),
             pltpu.VMEM((slots * 2 * pair_total, lat_count * head), BF),
             pltpu.VMEM((slots, 2 * degs, 2 * pair_total), BF),
-            pltpu.VMEM((slots, 2 * degs, width), BF),
-            pltpu.SemaphoreType.DMA,
             pltpu.SemaphoreType.DMA((lat_count,)),
             pltpu.SemaphoreType.DMA((lat_count,)),
             pltpu.SemaphoreType.DMA((lat_count,)),
@@ -308,9 +303,9 @@
             pltpu.SemaphoreType.DMA((lat_count,)),
         ],
         compiler_params=pltpu.CompilerParams(
-            collective_id=0, has_side_effects=True, vmem_limit_bytes=63 * 1024 * 1024
+            collective_id=0, has_side_effects=True, vmem_limit_bytes=52 * 1024 * 1024
         ),
-    )(x, basis, table, order_table.T, panel_modes)
+    )(*[pltpu.with_memory_space_constraint(v, pltpu.HBM) for v in (x, basis, table, order_table.T, panel_modes)])
     panel = lax.dot_general(
         coef.reshape(slots * 2 * degs, width), twice, NT, preferred_element_type=F32
     ) * (1.0 / (snap - 1))

time: 20.7 us -> 19.1 us (0.923)
  matrix products: 2.01 us -> 1.01 us
  Pallas kernels: 18.6 us -> 17.9 us
    dot_general x1, matrix products: 2.01 us -> 1.01 us  [fused(): lax.dot_general(coef.reshape(slots * 2 * degs, width), twice, NT, preferr...]
    pallas_call x1, Pallas kernels: 18.6 us -> 17.9 us  [fused(): pl.pallas_call(body, out_shape=(jax.ShapeDtypeStruct((slots, 2 * degs, wi...]
where the time goes in v4:
time: 19.1 us; the launch traced here: 18.9 us
  Pallas kernels  17.9 us (94%)
  matrix products  1.01 us (5%)
    pallas_call x1, Pallas kernels, fused(): pl.pallas_call(body, out_shape=(jax.ShapeDtypeStruct((slots, 2 * degs, wi...  17.9 us
    dot_general x1, matrix products, fused(): lax.dot_general(coef.reshape(slots * 2 * degs, width), twice, NT, preferr...  1.01 us

profile of v4, /device:TPU:1, one launch (start us, length us, event | category | flops | bytes accessed | tf_op | source)
XLA Modules:
  0.0 18.9 jit_solution(15908479888662236863)
XLA Ops:
  0.0 17.9 %shard_map.55 = (bf16[8,192,128]{2,1,0:T(8,128)(2,1)S(1)}, bf16[128,128]{1,0:T(8,128)(2,1)S(1)}) custom-call(bf16[64,3,2,192]{3,2,1,0:T(2,128)(2,1)} %bitcast.9, bf16[8,48,96]{2,1,0:T(8,128)(2,1)} %basis_hbm.1, bf16[192,768]{1,0:T(8,128)(2,1)} %constant.4.clone.table_hbm, s32[8,16]{1,0:T(8,128)} %bitcast.10, s32[2,64]{1,0:T(2,128)} %modes_hbm.1), custom_call_target="tpu_custom_call" | custom-call | tf_op jit(solution)/shard_map/pallas_call | solution.py:275
  17.9 1.0 %fusion = bf16[1536,128]{1,0:T(8,128)(2,1)} fusion(bf16[1536,128]{1,0:T(8,128)(2,1)S(1)} %bitcast.8, bf16[128,128]{1,0:T(8,128)(2,1)S(1)} %get-tuple-element.8), kind=kOutput, calls=%fused_computation.1 | convolution fusion | flops 50724864 | bytes 819200 | tf_op jit(solution)/shard_map/dot_general | solution.py:309

commit v5 on v4

--- a/solution.py
+++ b/solution.py
@@ -124,17 +124,24 @@
 
     pl.semaphore_wait(barrier, 2 * lat_count - 1)
 
+    def whole(src, dst, count, one_send_sem, one_recv_sem):
+        return pltpu.make_async_remote_copy(
+            src_ref=src.at[pl.ds(0, count)], dst_ref=dst.at[pl.ds(0, count)],
+            send_sem=one_send_sem, recv_sem=one_recv_sem,
+            device_id=(me, other), device_id_type=pl.DeviceIdType.MESH,
+        )
+
     def block_copy(dst, src):
         return pltpu.make_async_remote_copy(
             src_ref=send.at[dst], dst_ref=recv.at[src],
-            send_sem=send_sem.at[dst], recv_sem=recv_sem.at[src],
+            send_sem=send_sem, recv_sem=recv_sem,
             device_id=(dst, field), device_id_type=pl.DeviceIdType.MESH,
         )
 
     def tail_copy(dst, src):
         return pltpu.make_async_remote_copy(
             src_ref=tail_send.at[dst], dst_ref=tail_recv.at[src],
-            send_sem=tail_send_sem.at[dst], recv_sem=tail_recv_sem.at[src],
+            send_sem=tail_send_sem, recv_sem=tail_recv_sem,
             device_id=(dst, field), device_id_type=pl.DeviceIdType.MESH,
         )
 
@@ -157,7 +164,7 @@
     spread = (
         (iota((width, tail_rows), 0) == src_of * pairs + rho_of // per_dev) & (rho_of < used)
     ).astype(F32).astype(BF)
-    own_row = iota((tail, tail_rows), 0) - used == iota((tail, tail_rows), 1) % tail % per_dev
+    own_row = iota((per_dev, tail_rows), 0) == iota((per_dev, tail_rows), 1) % tail % per_dev
 
     k_rows = slots * 2 * pair_total
     for s in range(slots):
@@ -179,22 +186,18 @@
         even_part = jnp.where(keep & (odd == 0), base, 0.0)
         odd_part = jnp.where(keep & (odd == 1), base, 0.0)
         rows[s] = jnp.concatenate([even_part, odd_part], axis=1).astype(BF)
-    def wait_tail(k, c):
-        src = lax.rem(me + k, lat_count)
-        tail_copy(src, src).wait_recv()
-        return c
-
-    lax.fori_loop(1, lat_count, wait_tail, 0)
+    all_tails = whole(tail_send, tail_recv, lat_count - 1, tail_send_sem, tail_recv_sem)
+    all_tails.wait_recv()
 
     tails = tail_recv[...]
-    summed = jnp.sum(tails.astype(F32), axis=0).astype(BF)
+    summed = jnp.sum(tails.astype(F32), axis=0)[used:used + per_dev].astype(BF)
     weights = jnp.where(own_row, mm(summed, spread), 0.0).astype(BF)
     mode_send[...] = mm(weights, tails.reshape(tail_rows, width)).astype(BF)
 
     def mode_copy(dst, src):
         return pltpu.make_async_remote_copy(
             src_ref=mode_send, dst_ref=mode_recv.at[src],
-            send_sem=mode_send_sem.at[dst], recv_sem=mode_recv_sem.at[src],
+            send_sem=mode_send_sem, recv_sem=mode_recv_sem,
             device_id=(dst, other), device_id_type=pl.DeviceIdType.MESH,
         )
 
@@ -204,12 +207,8 @@
 
     lax.fori_loop(0, lat_count, start_mode, 0)
 
-    def wait_block(k, c):
-        src = lax.rem(me + k, lat_count)
-        block_copy(src, src).wait_recv()
-        return c
-
-    lax.fori_loop(1, lat_count, wait_block, 0)
+    all_blocks = whole(send, recv, lat_count - 1, send_sem, recv_sem)
+    all_blocks.wait_recv()
 
     heads = recv[...].reshape(lat_count * head, width)
     sorted_rows = mm(perm[...], heads).astype(BF)
@@ -219,17 +218,11 @@
         coef_hbm[s] = jnp.where(same_r, value, 0.0).astype(BF)
 
     modes = lat_count * per_dev
-    cu = iota((2 * modes, tail_rows), 0)
-    mode_at = cu // 2 // per_dev * tail + used + cu // 2 % per_dev
-    expand = (iota((2 * modes, tail_rows), 1) == mode_at).astype(F32).astype(BF)
-
-    def wait_mode(k, c):
-        src = lax.rem(me + k, lat_count)
-        mode_copy(src, src).wait_recv()
-        return c
-
-    lax.fori_loop(0, lat_count, wait_mode, 0)
-    values = mode_recv[...].reshape(tail_rows, width)
+    expand = (iota((2 * modes, modes), 1) == iota((2 * modes, modes), 0) // 2).astype(F32).astype(BF)
+
+    all_modes = whole(mode_recv, mode_recv, lat_count, mode_send_sem, mode_recv_sem)
+    all_modes.wait_recv()
+    values = mode_recv[...].reshape(modes, width)
     columns = mm(expand, values)
     u_match = iota((2 * modes, width), 1) // snap == iota((2 * modes, width), 0) % 2
     masked = jnp.where(u_match, columns, 0.0)
@@ -237,19 +230,9 @@
     centered = jnp.where(u_match, masked - mean, 0.0)
     twice_ref[...] = (centered + pltpu.roll(centered, snap, 1)).astype(BF)
 
-    def finish(k, c):
-        dst = lax.rem(me + k, lat_count)
-        block_copy(dst, dst).wait_send()
-        tail_copy(dst, dst).wait_send()
-        return c
-
-    def finish_mode(k, c):
-        dst = lax.rem(me + k, lat_count)
-        mode_copy(dst, dst).wait_send()
-        return c
-
-    lax.fori_loop(1, lat_count, finish, 0)
-    lax.fori_loop(0, lat_count, finish_mode, 0)
+    all_blocks.wait_send()
+    all_tails.wait_send()
+    all_modes.wait_send()
 
 
 def dft_constant(nord, lon):
@@ -291,16 +274,16 @@
             pltpu.VMEM((lat_count, head, width), BF),
             pltpu.VMEM((lat_count, tail, width), BF),
             pltpu.VMEM((lat_count, tail, width), BF),
-            pltpu.VMEM((tail, width), BF),
-            pltpu.VMEM((lat_count, tail, width), BF),
+            pltpu.VMEM((per_dev, width), BF),
+            pltpu.VMEM((lat_count, per_dev, width), BF),
             pltpu.VMEM((slots * 2 * pair_total, lat_count * head), BF),
             pltpu.VMEM((slots, 2 * degs, 2 * pair_total), BF),
-            pltpu.SemaphoreType.DMA((lat_count,)),
-            pltpu.SemaphoreType.DMA((lat_count,)),
-            pltpu.SemaphoreType.DMA((lat_count,)),
-            pltpu.SemaphoreType.DMA((lat_count,)),
-            pltpu.SemaphoreType.DMA((lat_count,)),
-            pltpu.SemaphoreType.DMA((lat_count,)),
+            pltpu.SemaphoreType.DMA,
+            pltpu.SemaphoreType.DMA,
+            pltpu.SemaphoreType.DMA,
+            pltpu.SemaphoreType.DMA,
+            pltpu.SemaphoreType.DMA,
+            pltpu.SemaphoreType.DMA,
         ],
         compiler_params=pltpu.CompilerParams(
             collective_id=0, has_side_effects=True, vmem_limit_bytes=52 * 1024 * 1024

time: 19.1 us -> 17.9 us (0.937)
  Pallas kernels: 17.9 us -> 16.7 us
    pallas_call x1, Pallas kernels: 17.9 us -> 16.7 us  [fused(): pl.pallas_call(body, out_shape=(jax.ShapeDtypeStruct((slots, 2 * degs, wi...]
where the time goes in v5:
time: 17.9 us; the launch traced here: 17.7 us
  Pallas kernels  16.7 us (93%)
  matrix products  1.01 us (6%)
    pallas_call x1, Pallas kernels, fused(): pl.pallas_call(body, out_shape=(jax.ShapeDtypeStruct((slots, 2 * degs, wi...  16.7 us
    dot_general x1, matrix products, fused(): lax.dot_general(coef.reshape(slots * 2 * degs, width), twice, NT, preferr...  1.01 us

profile of v5, /device:TPU:1, one launch (start us, length us, event | category | flops | bytes accessed | tf_op | source)
XLA Modules:
  0.0 17.7 jit_solution(6981113068866899363)
XLA Ops:
  0.0 16.7 %shard_map.55 = (bf16[8,192,128]{2,1,0:T(8,128)(2,1)S(1)}, bf16[128,128]{1,0:T(8,128)(2,1)S(1)}) custom-call(bf16[64,3,2,192]{3,2,1,0:T(2,128)(2,1)} %bitcast.9, bf16[8,48,96]{2,1,0:T(8,128)(2,1)} %basis_hbm.1, bf16[192,768]{1,0:T(8,128)(2,1)} %constant.4.clone.table_hbm, s32[8,16]{1,0:T(8,128)} %bitcast.10, s32[2,64]{1,0:T(2,128)} %modes_hbm.1), custom_call_target="tpu_custom_call" | custom-call | tf_op jit(solution)/shard_map/pallas_call | solution.py:258
  16.7 1.0 %fusion = bf16[1536,128]{1,0:T(8,128)(2,1)} fusion(bf16[1536,128]{1,0:T(8,128)(2,1)S(1)} %bitcast.8, bf16[128,128]{1,0:T(8,128)(2,1)S(1)} %get-tuple-element.8), kind=kOutput, calls=%fused_computation.1 | convolution fusion | flops 50724864 | bytes 819200 | tf_op jit(solution)/shard_map/dot_general | solution.py:292

commit v6 on v5

--- a/solution.py
+++ b/solution.py
@@ -138,6 +138,10 @@
             device_id=(dst, field), device_id_type=pl.DeviceIdType.MESH,
         )
 
+    def partner(step):
+        offset = lat_count // 2 + (1 - 2 * (step % 2)) * ((step + 1) // 2)
+        return lax.rem(me + offset, lat_count)
+
     def tail_copy(dst, src):
         return pltpu.make_async_remote_copy(
             src_ref=tail_send.at[dst], dst_ref=tail_recv.at[src],
@@ -146,16 +150,16 @@
         )
 
     def start_tail(k, c):
-        tail_copy(lax.rem(me + k, lat_count), me).start()
+        tail_copy(partner(k), me).start()
         return c
 
-    lax.fori_loop(1, lat_count, start_tail, 0)
+    lax.fori_loop(0, lat_count - 1, start_tail, 0)
 
     def start_block(k, c):
-        block_copy(lax.rem(me + k, lat_count), me).start()
+        block_copy(partner(k), me).start()
         return c
 
-    lax.fori_loop(1, lat_count, start_block, 0)
+    lax.fori_loop(0, lat_count - 1, start_block, 0)
     recv[me] = send[me]
     tail_recv[me] = tail_send[me]
 
@@ -202,7 +206,7 @@
         )
 
     def start_mode(k, c):
-        mode_copy(lax.rem(me + k, lat_count), me).start()
+        mode_copy(partner(k), me).start()
         return c
 
     lax.fori_loop(0, lat_count, start_mode, 0)
@@ -374,6 +378,7 @@
     rows = slots * 2 * pair_total
     fits = (
         modes % lat_count == 0
+        and lat_count % 2 == 0
         and tail == 2 * slots
         and tail % 16 == 0
         and 2 * snap == 128

time: 17.9 us -> 18 us (level)
  no operation moved by 1% of the time
where the time goes in v6:
time: 18 us; the launch traced here: 17.8 us
  Pallas kernels  16.8 us (93%)
  matrix products  1.01 us (6%)
    pallas_call x1, Pallas kernels, fused(): pl.pallas_call(body, out_shape=(jax.ShapeDtypeStruct((slots, 2 * degs, wi...  16.8 us
    dot_general x1, matrix products, fused(): lax.dot_general(coef.reshape(slots * 2 * degs, width), twice, NT, preferr...  1.01 us

profile of v6, /device:TPU:1, one launch (start us, length us, event | category | flops | bytes accessed | tf_op | source)
XLA Modules:
  0.0 17.8 jit_solution(5372619854679192085)
XLA Ops:
  0.0 16.8 %shard_map.55 = (bf16[8,192,128]{2,1,0:T(8,128)(2,1)S(1)}, bf16[128,128]{1,0:T(8,128)(2,1)S(1)}) custom-call(bf16[64,3,2,192]{3,2,1,0:T(2,128)(2,1)} %bitcast.9, bf16[8,48,96]{2,1,0:T(8,128)(2,1)} %basis_hbm.1, bf16[192,768]{1,0:T(8,128)(2,1)} %constant.4.clone.table_hbm, s32[8,16]{1,0:T(8,128)} %bitcast.10, s32[2,64]{1,0:T(2,128)} %modes_hbm.1), custom_call_target="tpu_custom_call" | custom-call | tf_op jit(solution)/shard_map/pallas_call | solution.py:262
  16.8 1.0 %fusion = bf16[1536,128]{1,0:T(8,128)(2,1)} fusion(bf16[1536,128]{1,0:T(8,128)(2,1)S(1)} %bitcast.8, bf16[128,128]{1,0:T(8,128)(2,1)S(1)} %get-tuple-element.8), kind=kOutput, calls=%fused_computation.1 | convolution fusion | flops 50724864 | bytes 819200 | tf_op jit(solution)/shard_map/dot_general | solution.py:296

commit v7 on v5

--- a/solution.py
+++ b/solution.py
@@ -100,6 +100,7 @@
     match = (mode_col == row_order) & (mode_parity == row_parity)
     tail_acc = jnp.zeros((tail_rows, width), F32)
     zero_x = jnp.zeros((snap, 2 * lon), BF)
+    parts = []
     loads[3].wait()
     for j in range(pairs):
         xj = jnp.concatenate([x_ref[:, j, 0, :], x_ref[:, j, 1, :]], axis=1)
@@ -108,8 +109,10 @@
         )
         part = (mm_nt(dft, both) * (1.0 / math.sqrt(lon))).astype(BF)
         send[:, j * block:(j + 1) * block, :] = part.reshape(lat_count, block, width)
-        mine = match & (rho // per_dev == j)
-        tail_acc = tail_acc + mm(mine.astype(F32).astype(BF), part)
+        parts.append(part)
+    picked = mm(match.astype(F32).astype(BF), jnp.concatenate(parts, axis=1))
+    for j in range(pairs):
+        tail_acc = jnp.where(rho // per_dev == j, picked[:, j * width:(j + 1) * width], tail_acc)
     at_degree = (iota((tail_rows, degs), 1) == deg_col) & (rho >= used) & (rho < used + per_dev)
     loads[4].wait()
     basis_acc = jnp.zeros((tail_rows, pair_total), F32)

time: 17.9 us -> 17.9 us (level)
  no operation moved by 1% of the time
where the time goes in v7:
time: 17.9 us; the launch traced here: 17.7 us
  Pallas kernels  16.7 us (93%)
  matrix products  1.01 us (6%)
    pallas_call x1, Pallas kernels, fused(): pl.pallas_call(body, out_shape=(jax.ShapeDtypeStruct((slots, 2 * degs, wi...  16.7 us
    dot_general x1, matrix products, fused(): lax.dot_general(coef.reshape(slots * 2 * degs, width), twice, NT, preferr...  1.01 us

profile of v7, /device:TPU:1, one launch (start us, length us, event | category | flops | bytes accessed | tf_op | source)
XLA Modules:
  0.0 17.7 jit_solution(325378484383481696)
XLA Ops:
  0.0 16.7 %shard_map.55 = (bf16[8,192,128]{2,1,0:T(8,128)(2,1)S(1)}, bf16[128,128]{1,0:T(8,128)(2,1)S(1)}) custom-call(bf16[64,3,2,192]{3,2,1,0:T(2,128)(2,1)} %bitcast.9, bf16[8,48,96]{2,1,0:T(8,128)(2,1)} %basis_hbm.1, bf16[192,768]{1,0:T(8,128)(2,1)} %constant.4.clone.table_hbm, s32[8,16]{1,0:T(8,128)} %bitcast.10, s32[2,64]{1,0:T(2,128)} %modes_hbm.1), custom_call_target="tpu_custom_call" | custom-call | tf_op jit(solution)/shard_map/pallas_call | solution.py:261
  16.7 1.0 %fusion = bf16[1536,128]{1,0:T(8,128)(2,1)} fusion(bf16[1536,128]{1,0:T(8,128)(2,1)S(1)} %bitcast.8, bf16[128,128]{1,0:T(8,128)(2,1)S(1)} %get-tuple-element.8), kind=kOutput, calls=%fused_computation.1 | convolution fusion | flops 50724864 | bytes 819200 | tf_op jit(solution)/shard_map/dot_general | solution.py:295
